TPU v7x, 32 devices: a whole 2x2x4 slice. The times are simulated.
32 devices in a mesh: grp: 4 (over y, x), dev: 8 (over z, core).
Axes of the slice: x: 2, y: 2, z: 4, core: 2. Of those that a mesh axis runs over, the one named last changes fastest.
Arguments:
- tokens: bfloat16 [8192, 1024], P(('grp', 'dev')), may hold values from -6 to 6
- cotangent: bfloat16 [8192, 1024], P(('grp', 'dev')), may hold values from -6 to 6
- lengths: int32 [8], replicated, may hold values from 256 to 1024, as said below
- offsets: int32 [8], replicated, may hold values from 0 to 768, as said below
- ln_gain: bfloat16 [1024], P(('grp', 'dev')), may hold values from 0.5 to 1.5
- ln_bias: bfloat16 [1024], P(('grp', 'dev')), may hold values from -2 to 2
- w_qkv: bfloat16 [1024, 3072], P(('grp', 'dev')), may hold values from -0.1875 to 0.1875
- w_out: bfloat16 [1024, 1024], P(('grp', 'dev')), may hold values from -3 to 3
- w_fc1: bfloat16 [1024, 4096], P(('grp', 'dev')), may hold values from -0.1875 to 0.1875
- b_fc1: bfloat16 [4096], P(('grp', 'dev')), may hold values from -2 to 2
- w_fc2: bfloat16 [4096, 1024], P(('grp', 'dev')), may hold values from -0.09375 to 0.09375
- b_fc2: bfloat16 [1024], P(('grp', 'dev')), may hold values from -2 to 2
Outputs:
- mixed: bfloat16 [8192, 1024], P(('grp', 'dev'))
- token_grad: bfloat16 [8192, 1024], P(('grp', 'dev'))
- g_ln_gain: float32 [1024], P('dev')
- g_ln_bias: float32 [1024], P('dev')
- g_w_qkv: float32 [1024, 3072], P('dev')
- g_w_out: float32 [1024, 1024], P('dev')
- g_w_fc1: float32 [1024, 4096], P('dev')
- g_b_fc1: float32 [4096], P('dev')
- g_w_fc2: float32 [4096, 1024], P('dev')
- g_b_fc2: float32 [1024], P('dev')
Inputs may be any that keep to these rules, and one draw needn't show every extreme that they name: `lengths`: one slot in every draw has length 1024 and one has 256. offsets + lengths <= 1024; one slot of length 256 ends at place 1024 - 1.
All inputs are finite; a program needn't handle non-finite values.
Results may differ from a plain program's by a relative error of at most 0.015.
Values may be sent and summed in bfloat16 or wider, within the bound.
A program may use at most 192 MiB of HBM per device.

v0:
```python
import math
import jax
import jax.numpy as jnp
from jax import lax
from jax.sharding import PartitionSpec as P

HEADS = 16
ROT = 32
DPS = 4


def swapped(array, axis, distance):
    return lax.ppermute(array, axis, [(i, i ^ 1 << distance) for i in range(lax.axis_size(axis))])


def gelu_tanh(values_in):
    return (
        0.5
        * values_in
        * (
            1.0
            + jnp.tanh(
                0.7978845608028654 * (values_in + 0.044715 * values_in * values_in * values_in)
            )
        )
    )


def gelu_slope(values_in):
    tangent = jnp.tanh(
        0.7978845608028654 * (values_in + 0.044715 * values_in * values_in * values_in)
    )
    inner_slope = 0.7978845608028654 * (1.0 + 0.134145 * values_in * values_in)
    return 0.5 * (1.0 + tangent) + 0.5 * values_in * (1.0 - tangent * tangent) * inner_slope


def turn_tables(places):
    half_rot = ROT // 2
    frequency = jnp.exp(jnp.arange(half_rot, dtype=jnp.float32) * (-2.0 * math.log(10000.0) / ROT))
    angles = places[:, None] * frequency[None, :]
    return (jnp.cos(angles)[:, None, :], jnp.sin(angles)[:, None, :])


def rotate(field_in, cosine, sine_table):
    half_rot = ROT // 2
    first_half = field_in[..., :half_rot]
    second = field_in[..., half_rot:ROT]
    return jnp.concatenate(
        [
            first_half * cosine - second * sine_table,
            second * cosine + first_half * sine_table,
            field_in[..., ROT:],
        ],
        axis=-1,
    )


def rotate_back(field_in, cosine, sine_table):
    half_rot = ROT // 2
    first_half = field_in[..., :half_rot]
    second = field_in[..., half_rot:ROT]
    return jnp.concatenate(
        [
            first_half * cosine + second * sine_table,
            second * cosine - first_half * sine_table,
            field_in[..., ROT:],
        ],
        axis=-1,
    )


def place_of(local_rows, row_count, slot_len):
    piece = local_rows // row_count
    inner = local_rows % row_count
    half_rows = row_count // 2
    return jnp.where(
        inner < half_rows,
        piece * half_rows + inner,
        slot_len - (piece + 1) * half_rows + (inner - half_rows),
    )


def allowed_table(query_places, key_places, offset, length):
    live_keys = (key_places >= offset) & (key_places < offset + length)
    return (key_places[None, :] <= query_places[:, None]) & (
        live_keys[None, :] | (key_places[None, :] == query_places[:, None])
    )


def attend_forward(queries, key_stack, value_stack, allowed):
    head_size = queries.shape[2]
    score_scale = 1.0 / math.sqrt(head_size)
    head_group = math.gcd(HEADS, 4)
    outputs = []
    maxima = []
    for first_head in range(0, HEADS, head_group):
        part_query = queries[:, first_head : first_head + head_group]
        part_keys = key_stack[:, first_head : first_head + head_group]
        part_values = value_stack[:, first_head : first_head + head_group]
        scores = (
            jnp.einsum("qhd,khd->hqk", part_query, part_keys, preferred_element_type=jnp.float32)
            * score_scale
        )
        scores = jnp.where(allowed[None], scores, -1e30)
        row_max = jnp.max(scores, axis=-1, keepdims=True)
        expo = jnp.exp(scores - row_max)
        denom = jnp.sum(expo, axis=-1, keepdims=True)
        probs_low = (expo / denom).astype(jnp.bfloat16)
        outputs.append(
            jnp.einsum("hqk,khd->qhd", probs_low, part_values, preferred_element_type=jnp.float32)
        )
        maxima.append((row_max + jnp.log(denom))[..., 0])
    return (jnp.concatenate(outputs, axis=1), jnp.concatenate(maxima, axis=0))


def attend_backward(queries, key_stack, value_stack, grad_att, log_total, allowed):
    head_size = queries.shape[2]
    score_scale = 1.0 / math.sqrt(head_size)
    head_group = math.gcd(HEADS, 4)
    grad_q_parts = []
    grad_k_parts = []
    grad_v_parts = []
    for first_head in range(0, HEADS, head_group):
        part_query = queries[:, first_head : first_head + head_group]
        part_keys = key_stack[:, first_head : first_head + head_group]
        part_values = value_stack[:, first_head : first_head + head_group]
        part_grad = grad_att[:, first_head : first_head + head_group]
        part_total = log_total[first_head : first_head + head_group]
        scores = (
            jnp.einsum("qhd,khd->hqk", part_query, part_keys, preferred_element_type=jnp.float32)
            * score_scale
        )
        scores = jnp.where(allowed[None], scores, -1e30)
        probs = jnp.exp(scores - part_total[:, :, None])
        probs_low = probs.astype(jnp.bfloat16)
        grad_v_parts.append(
            jnp.einsum("hqk,qhd->khd", probs_low, part_grad, preferred_element_type=jnp.float32)
        )
        grad_prob = jnp.einsum(
            "qhd,khd->hqk", part_grad, part_values, preferred_element_type=jnp.float32
        )
        row_dot = jnp.sum(probs * grad_prob, axis=-1, keepdims=True)
        grad_score = (probs * (grad_prob - row_dot)).astype(jnp.bfloat16)
        grad_q_parts.append(
            jnp.einsum("hqk,khd->qhd", grad_score, part_keys, preferred_element_type=jnp.float32)
            * score_scale
        )
        grad_k_parts.append(
            jnp.einsum("hqk,qhd->khd", grad_score, part_query, preferred_element_type=jnp.float32)
            * score_scale
        )
    return (
        jnp.concatenate(grad_q_parts, axis=1),
        jnp.concatenate(grad_k_parts, axis=1),
        jnp.concatenate(grad_v_parts, axis=1),
    )


def local(
    tokens, cotangent, lengths, offsets, ln_gain, ln_bias, w_qkv, w_out, w_fc1, b_fc1, w_fc2, b_fc2
):
    row_count = tokens.shape[0]
    width = tokens.shape[1]
    head_size = width // HEADS
    slot_len = row_count * DPS
    bit_count = DPS.bit_length() - 1
    dev_count = lax.axis_size("dev")
    dev_index = lax.axis_index("dev")
    first_row = (lax.axis_index("grp") * dev_count + dev_index) * row_count
    slot_index = first_row // slot_len
    slot_piece = first_row % slot_len // row_count
    length = lengths[slot_index]
    offset = offsets[slot_index]
    query_places = place_of(
        slot_piece * row_count + jnp.arange(row_count, dtype=jnp.int32), row_count, slot_len
    )
    key_places = place_of(jnp.arange(slot_len, dtype=jnp.int32), row_count, slot_len)
    live_rows = (query_places >= offset) & (query_places < offset + length)
    live_float = live_rows.astype(jnp.float32)[:, None]
    cosine, sine_table = turn_tables((query_places - offset).astype(jnp.float32))
    allowed = allowed_table(query_places, key_places, offset, length)
    gathered = (
        lax.all_gather(ln_gain, ("grp", "dev"), axis=0, tiled=True),
        lax.all_gather(ln_bias, ("grp", "dev"), axis=0, tiled=True),
        lax.all_gather(w_qkv, ("grp", "dev"), axis=0, tiled=True),
        lax.all_gather(w_out, ("grp", "dev"), axis=0, tiled=True),
        lax.all_gather(w_fc1, ("grp", "dev"), axis=0, tiled=True),
        lax.all_gather(b_fc1, ("grp", "dev"), axis=0, tiled=True),
        lax.all_gather(w_fc2, ("grp", "dev"), axis=0, tiled=True),
        lax.all_gather(b_fc2, ("grp", "dev"), axis=0, tiled=True),
    )
    full_gain, full_bias, full_qkv, full_out, full_fc1, full_bfc1, full_fc2, full_bfc2 = gathered
    norm_gain = full_gain.astype(jnp.float32)
    tokens_f = tokens.astype(jnp.float32)
    centred = tokens_f - jnp.mean(tokens_f, axis=-1, keepdims=True)
    inverse = lax.rsqrt(jnp.mean(centred * centred, axis=-1, keepdims=True) + 1e-05)
    normed = centred * inverse
    hidden_low = (normed * norm_gain + full_bias.astype(jnp.float32)).astype(jnp.bfloat16)
    mixed_qkv = jnp.dot(hidden_low, full_qkv, preferred_element_type=jnp.float32)
    queries = rotate(
        mixed_qkv[:, :width].reshape(row_count, HEADS, head_size), cosine, sine_table
    ).astype(jnp.bfloat16)
    key_rows = rotate(
        mixed_qkv[:, width : 2 * width].reshape(row_count, HEADS, head_size), cosine, sine_table
    ).astype(jnp.bfloat16)
    value_rows = mixed_qkv[:, 2 * width :].astype(jnp.bfloat16)
    blocks = jnp.stack([key_rows.reshape(row_count, width), value_rows])[:, None]
    for bit in range(bit_count):
        partner = swapped(blocks, "dev", bit)
        upper = dev_index // (1 << bit) % 2 == 1
        blocks = jnp.where(
            upper,
            jnp.concatenate([partner, blocks], axis=1),
            jnp.concatenate([blocks, partner], axis=1),
        )
    key_stack = blocks[0].reshape(slot_len, HEADS, head_size)
    value_stack = blocks[1].reshape(slot_len, HEADS, head_size)
    attended, log_total = attend_forward(queries, key_stack, value_stack, allowed)
    attended_low = attended.reshape(row_count, width).astype(jnp.bfloat16)
    pre_act = jnp.dot(hidden_low, full_fc1, preferred_element_type=jnp.float32) + full_bfc1.astype(
        jnp.float32
    )
    act_low = gelu_tanh(pre_act).astype(jnp.bfloat16)
    attn_part = jnp.dot(attended_low, full_out, preferred_element_type=jnp.float32)
    mlp_part = jnp.dot(act_low, full_fc2, preferred_element_type=jnp.float32) + full_bfc2.astype(
        jnp.float32
    )
    mixed = (live_float * (tokens_f + attn_part + mlp_part)).astype(jnp.bfloat16)
    back_gain, back_qkv, back_out, back_fc1, back_fc2 = (
        lax.all_gather(ln_gain, ("grp", "dev"), axis=0, tiled=True),
        lax.all_gather(w_qkv, ("grp", "dev"), axis=0, tiled=True),
        lax.all_gather(w_out, ("grp", "dev"), axis=0, tiled=True),
        lax.all_gather(w_fc1, ("grp", "dev"), axis=0, tiled=True),
        lax.all_gather(w_fc2, ("grp", "dev"), axis=0, tiled=True),
    )
    back_gain = back_gain.astype(jnp.float32)
    grad_y = cotangent.astype(jnp.float32) * live_float
    grad_low = grad_y.astype(jnp.bfloat16)
    g_w_out = jnp.einsum("rd,re->de", attended_low, grad_low, preferred_element_type=jnp.float32)
    g_b_fc2 = jnp.sum(grad_y, axis=0)
    g_w_fc2 = jnp.einsum("rf,re->fe", act_low, grad_low, preferred_element_type=jnp.float32)
    grad_act = jnp.einsum("re,fe->rf", grad_low, back_fc2, preferred_element_type=jnp.float32)
    grad_pre = (grad_act * gelu_slope(pre_act)).astype(jnp.bfloat16)
    g_w_fc1 = jnp.einsum("rd,rf->df", hidden_low, grad_pre, preferred_element_type=jnp.float32)
    g_b_fc1 = jnp.sum(grad_pre.astype(jnp.float32), axis=0)
    grad_h = jnp.einsum("rf,df->rd", grad_pre, back_fc1, preferred_element_type=jnp.float32)
    grad_att = jnp.einsum(
        "re,de->rd", grad_low, back_out, preferred_element_type=jnp.float32
    ).astype(jnp.bfloat16)
    grad_query, grad_keys, grad_values = attend_backward(
        queries,
        key_stack,
        value_stack,
        grad_att.reshape(row_count, HEADS, head_size),
        log_total,
        allowed,
    )
    back_blocks = jnp.stack(
        [grad_keys.reshape(slot_len, width), grad_values.reshape(slot_len, width)]
    ).reshape(2, DPS, row_count, width)
    for bit in range(bit_count - 1, -1, -1):
        count_now = back_blocks.shape[1] // 2
        lower_half = back_blocks[:, :count_now]
        upper_half = back_blocks[:, count_now:]
        upper = dev_index // (1 << bit) % 2 == 1
        kept = jnp.where(upper, upper_half, lower_half)
        outgoing = jnp.where(upper, lower_half, upper_half)
        back_blocks = kept + swapped(outgoing, "dev", bit)
    own_keys = back_blocks[0, 0]
    own_values = back_blocks[1, 0]
    grad_q_pre = rotate_back(grad_query, cosine, sine_table).reshape(row_count, width)
    grad_k_pre = rotate_back(
        own_keys.reshape(row_count, HEADS, head_size), cosine, sine_table
    ).reshape(row_count, width)
    grad_qkv = jnp.concatenate([grad_q_pre, grad_k_pre, own_values], axis=1).astype(jnp.bfloat16)
    g_w_qkv = jnp.einsum("rd,re->de", hidden_low, grad_qkv, preferred_element_type=jnp.float32)
    grad_h = grad_h + jnp.einsum(
        "re,de->rd", grad_qkv, back_qkv, preferred_element_type=jnp.float32
    )
    g_ln_gain = jnp.sum(grad_h * normed, axis=0)
    g_ln_bias = jnp.sum(grad_h, axis=0)
    scaled_grad = grad_h * back_gain
    grad_norm = inverse * (
        scaled_grad
        - jnp.mean(scaled_grad, axis=-1, keepdims=True)
        - normed * jnp.mean(scaled_grad * normed, axis=-1, keepdims=True)
    )
    token_grad = (grad_y + grad_norm).astype(jnp.bfloat16)
    gradients = (g_ln_gain, g_ln_bias, g_w_qkv, g_w_out, g_w_fc1, g_b_fc1, g_w_fc2, g_b_fc2)
    shares = (
        lax.psum_scatter(
            gradients[0].astype(jnp.bfloat16), "dev", scatter_dimension=0, tiled=True
        ).astype(jnp.float32),
        lax.psum_scatter(
            gradients[1].astype(jnp.bfloat16), "dev", scatter_dimension=0, tiled=True
        ).astype(jnp.float32),
        lax.psum_scatter(
            gradients[2].astype(jnp.bfloat16), "dev", scatter_dimension=0, tiled=True
        ).astype(jnp.float32),
        lax.psum_scatter(
            gradients[3].astype(jnp.bfloat16), "dev", scatter_dimension=0, tiled=True
        ).astype(jnp.float32),
        lax.psum_scatter(
            gradients[4].astype(jnp.bfloat16), "dev", scatter_dimension=0, tiled=True
        ).astype(jnp.float32),
        lax.psum_scatter(
            gradients[5].astype(jnp.bfloat16), "dev", scatter_dimension=0, tiled=True
        ).astype(jnp.float32),
        lax.psum_scatter(
            gradients[6].astype(jnp.bfloat16), "dev", scatter_dimension=0, tiled=True
        ).astype(jnp.float32),
        lax.psum_scatter(
            gradients[7].astype(jnp.bfloat16), "dev", scatter_dimension=0, tiled=True
        ).astype(jnp.float32),
    )
    summed = (
        lax.psum(shares[0].astype(jnp.bfloat16), "grp").astype(jnp.float32),
        lax.psum(shares[1].astype(jnp.bfloat16), "grp").astype(jnp.float32),
        lax.psum(shares[2].astype(jnp.bfloat16), "grp").astype(jnp.float32),
        lax.psum(shares[3].astype(jnp.bfloat16), "grp").astype(jnp.float32),
        lax.psum(shares[4].astype(jnp.bfloat16), "grp").astype(jnp.float32),
        lax.psum(shares[5].astype(jnp.bfloat16), "grp").astype(jnp.float32),
        lax.psum(shares[6].astype(jnp.bfloat16), "grp").astype(jnp.float32),
        lax.psum(shares[7].astype(jnp.bfloat16), "grp").astype(jnp.float32),
    )
    return (mixed, token_grad) + tuple(summed)


def solution(mesh):
    return jax.shard_map(
        local,
        mesh=mesh,
        in_specs=(
            P(("grp", "dev"), None),
            P(("grp", "dev"), None),
            P(),
            P(),
            P(("grp", "dev")),
            P(("grp", "dev")),
            P(("grp", "dev"), None),
            P(("grp", "dev"), None),
            P(("grp", "dev"), None),
            P(("grp", "dev")),
            P(("grp", "dev"), None),
            P(("grp", "dev")),
        ),
        out_specs=(
            P(("grp", "dev"), None),
            P(("grp", "dev"), None),
            P("dev"),
            P("dev"),
            P("dev", None),
            P("dev", None),
            P("dev", None),
            P("dev"),
            P("dev", None),
            P("dev"),
        ),
        check_vma=False,
    )
```

profile of v0, /device:TPU:0, one launch (start us, length us, event | category | flops | bytes accessed | tf_op | source)
XLA Modules:
  0.0 792.3 jit_solution(6765322636481741186)
XLA Ops:
  12.6 42.5 %all-reduce.7 = (bf16[1024]{0:T(1024)(128)(2,1)}, bf16[1024]{0:T(1024)(128)(2,1)S(1)}, bf16[1024]{0:T(1024)(128)(2,1)S(1)}) all-reduce(bf16[1024]{0:T(1024)(128)(2,1)S(1)} %dynamic-update-slice.2, bf16[1024]{0:T(1024)(128)(2,1)S(1)} %dynamic-update-slice.1, ...), channel_id=1, replica_groups=mesh['grp'=4,'dev'=8] {'grp','dev'}, use_global_device_ids=true, to_apply=%add.2 | all-reduce | flops 3072 | bytes 12288
  55.1 1.2 dynamic_slice.6
  58.8 1.5 fusion.76
  61.0 22.3 %all-gather.6.cloned.1.call-done = bf16[1024,3072]{1,0:T(8,128)(2,1)} async-done(((bf16[32,3072]{1,0:T(8,128)(2,1)}), bf16[1024,3072]{1,0:T(8,128)(2,1)}) %all-gather.6.cloned.1.call-update) | async-done | bytes 6291472 | tf_op jit(solution)/shard_map/all_gather | solution.py:185
  83.4 4.9 fusion.118
  88.4 1.5 copy-done.26
  90.6 1.5 subtract_convert_fusion.2
  92.4 1.3 fusion.79
  94.2 2.5 collective-permute-done
  96.8 1.9 maximum_select_fusion.1
  98.6 1.4 collective-permute-start.1
  104.8 78.3 %collective-permute-done.1 = bf16[2,2,256,1024]{3,2,0,1:T(8,128)(2,1)} collective-permute-done((bf16[2,2,256,1024]{3,2,0,1:T(8,128)(2,1)S(1)}, bf16[2,2,256,1024]{3,2,0,1:T(8,128)(2,1)}, u32[]{:S(2)}, u32[]{:S(2)}) %collective-permute-start.1) | collective-permute-done | bytes 2097184 | tf_op jit(solution)/shard_map/ppermute | solution.py:13
  183.1 2.5 maximum_select_fusion
  185.6 2.4 fusion.120
  188.1 3.0 copy.55
  191.1 2.7 reshape_squeeze.10
  193.8 3.1 copy.53
  196.9 2.9 reshape_squeeze.9
  199.8 2.2 fusion.122
  203.1 2.0 copy-done.27
  211.7 2.0 copy-done.18
  218.9 2.2 convolution_convert_fusion.3
  221.2 40.2 %all-gather = bf16[32,1,128]{2,1,0:T(2,128)(2,1)S(1)} all-gather(bf16[1,1,128]{2,1,0:T(2,128)(2,1)} %bitcast.117), channel_id=1, replica_groups=mesh['grp'=4,'dev'=8] {'grp','dev'}, dimensions={0}, use_global_device_ids=true | all-gather | bytes 8448 | tf_op jit(solution)/shard_map/all_gather | solution.py:188
  262.0 5.9 convolution_add_fusion
  267.9 2.0 copy-done.63
  269.8 5.5 convolution_convert_fusion
  275.4 3.2 convolution_convert_fusion.4
  278.6 1.2 copy.56
  281.9 4.0 fusion.40
  285.9 35.7 %all-gather.12.cloned.1.call-done = bf16[4096,1024]{1,0:T(8,128)(2,1)} async-done(((bf16[128,1024]{1,0:T(8,128)(2,1)}), bf16[4096,1024]{1,0:T(8,128)(2,1)}) %all-gather.12.cloned.1.call-update) | async-done | bytes 8388624 | tf_op jit(solution)/shard_map/all_gather | solution.py:189
  321.6 8.2 %fusion.126 = (bf16[4096]{0:T(1024)(128)(2,1)}, bf16[256,4096]{1,0:T(8,128)(2,1)S(1)}) fusion(f32[256,4096]{1,0:T(8,128)} %copy-done.63, bf16[4096,1024]{1,0:T(8,128)(2,1)} %all-gather.12.cloned.1.call-done, bf16[256,1024]{1,0:T(8,128)(2,1)} %param.13, f32[256]{0:T(256)} %copy-done.41), kind=kOutput, calls=%fused_computation.212 | convolution fusion | flops 2169237504 | bytes 15213568 | tf_op jit(solution)/shard_map/re,fe->rf/dot_general | solution.py:242
  329.8 1.3 copy-done.30
  331.1 5.8 convolution_convert_fusion.1
  337.8 3.2 fusion.37
  341.9 1.4 copy-done.6
  344.5 2.6 pad_maximum_fusion.1
  347.1 5.8 stack.16
  352.9 3.9 multiply_reduce_fusion
  359.7 1.6 multiply_reduce_fusion.1
  362.7 1.6 copy-done.7
  364.3 1.6 multiply_reduce_fusion.3
  367.2 1.6 copy-done.2
  368.8 1.6 multiply_reduce_fusion.2
  371.3 1.3 copy-done.16
  373.1 2.5 pad_maximum_fusion
  375.6 5.8 stack.15
  381.5 3.1 copy_dynamic-update-slice_fusion.1
  386.7 1.6 collective-permute-start.2
  388.3 168.8 %collective-permute-done.2 = f32[2,2,256,1024]{2,3,1,0:T(8,128)S(1)} collective-permute-done((f32[2,2,256,1024]{2,3,1,0:T(8,128)S(1)}, f32[2,2,256,1024]{2,3,1,0:T(8,128)S(1)}, u32[]{:S(2)}, u32[]{:S(2)}) %collective-permute-start.2) | collective-permute-done | bytes 4194336 | tf_op jit(solution)/shard_map/ppermute | solution.py:13
  565.5 4.6 convolution_convert_fusion.2
  572.8 44.7 %reduce-scatter.9.cloned.1.call-done = bf16[128,4096]{1,0:T(8,128)(2,1)} async-done(((bf16[1024,4096]{1,0:T(8,128)(2,1)}), bf16[128,4096]{1,0:T(8,128)(2,1)}) %reduce-scatter.9.cloned.1.call-update) | async-done | bytes 1048592 | tf_op jit(solution)/shard_map/reduce_scatter | solution.py:303
  617.5 70.2 %reduce-scatter.5.cloned.1.call-done = bf16[128,3072]{1,0:T(8,128)(2,1)} async-done(((bf16[1024,3072]{1,0:T(8,128)(2,1)}), bf16[128,3072]{1,0:T(8,128)(2,1)}) %reduce-scatter.5.cloned.1.call-update) | async-done | bytes 786448 | tf_op jit(solution)/shard_map/reduce_scatter | solution.py:297
  687.8 7.5 convolution_add_fusion.2
  695.4 1.5 fusion.49
  697.1 5.7 fusion.127
  702.8 5.1 fusion.75
  708.0 1.3 fusion.77
  709.3 26.8 %all-reduce.8 = (bf16[1024]{0:T(1024)(128)(2,1)S(1)}, bf16[1024]{0:T(1024)(128)(2,1)S(1)}, bf16[4096]{0:T(1024)(128)(2,1)S(1)}, bf16[1024]{0:T(1024)(128)(2,1)S(1)}) all-reduce(bf16[1024]{0:T(1024)(128)(2,1)S(1)} %get-tuple-element.10, bf16[1024]{0:T(1024)(128)(2,1)S(1)} %get-tuple-element.13, ...), channel_id=2, replica_groups=mesh['grp'=4,'dev'=8] {'dev'}, use_global_device_ids=true, to_apply=%region_17.18.clone | all-reduce | flops 7168 | bytes 28672
  736.4 10.5 %all-reduce.9 = (bf16[128]{0:T(256)(128)(2,1)S(1)}, bf16[128]{0:T(256)(128)(2,1)S(1)}, bf16[512]{0:T(512)(128)(2,1)S(1)}, bf16[128]{0:T(256)(128)(2,1)S(1)}) all-reduce(bf16[128]{0:T(256)(128)(2,1)S(1)} %dynamic-slice.1, bf16[128]{0:T(256)(128)(2,1)S(1)} %dynamic-slice.3, ...), channel_id=1, replica_groups=mesh['grp'=4,'dev'=8] {'grp'}, use_global_device_ids=true, to_apply=%region_18.19 | all-reduce | flops 896 | bytes 3584 | tf_op jit(solution)/shard_map/psum | solution.py:317
  749.0 27.6 %all-reduce.13.cloned.1.call-done = (bf16[128,3072]{1,0:T(8,128)(2,1)}, bf16[128,1024]{1,0:T(8,128)(2,1)}, bf16[128,4096]{1,0:T(8,128)(2,1)}, bf16[512,1024]{1,0:T(8,128)(2,1)}) async-done(((bf16[128,3072]{1,0:T(8,128)(2,1)}, bf16[128,1024]{1,0:T(8,128)(2,1)}, bf16[128,4096]{1,0:T(8,128)(2,1)}, bf16[512,1024]{1,0:T(8,128)(2,1)}), (bf16[128,3072]{1,0:T(8,128)(2,1)}, bf16[128,1024]{1,0:T(8,128)(2,1)}, ...) | async-done | bytes 3145744 | tf_op jit(solution)/shard_map/psum | solution.py:319
  776.7 1.9 convert_element_type.207
  778.5 2.4 convert_element_type.205
  781.0 2.8 convert_element_type.209
  783.7 1.6 convert_element_type.212
  (227 shorter events, 53.0 us)
Async XLA Ops:
  7.2 76.2 %all-gather.6.cloned.1.call-start = ((), (), s32[]{:S(2)}) async-start(), calls=%async_computation.4 | async-start | bytes 6488064 | tf_op jit(solution)/shard_map/all_gather | solution.py:185
  7.9 254.1 %all-gather.10.cloned.1.call-start = ((), (), s32[]{:S(2)}) async-start(), calls=%async_computation.6 | async-start | bytes 8650752 | tf_op jit(solution)/shard_map/all_gather | solution.py:187
  8.7 266.7 %all-gather.8.cloned.1.call-start = ((), (), s32[]{:S(2)}) async-start(), calls=%async_computation.5 | async-start | bytes 2162688 | tf_op jit(solution)/shard_map/all_gather | solution.py:186
  9.4 312.2 %all-gather.12.cloned.1.call-start = ((), (), s32[]{:S(2)}) async-start(), calls=%async_computation.7 | async-start | bytes 8650752 | tf_op jit(solution)/shard_map/all_gather | solution.py:189
  10.0 562.8 %reduce-scatter.7.cloned.1.call-start = ((), (), s32[]{:S(2)}) async-start(), calls=%async_computation.9 | async-start | bytes 2359296 | tf_op jit(solution)/shard_map/reduce_scatter | solution.py:300
  58.7 203.2 %copy-start.43 = (f32[256]{0:T(256)}, f32[256]{0:T(256)S(1)}, u32[]{:S(2)}) copy-start(f32[256]{0:T(256)S(1)} %broadcast_multiply_fusion.2) | copy-start | bytes 3076
  60.2 28.0 %copy-start.46 = (f32[256]{0:T(256)}, f32[256]{0:T(256)S(1)}, u32[]{:S(2)}) copy-start(f32[256]{0:T(256)S(1)} %add_rsqrt_fusion) | copy-start | bytes 3076
  88.2 1.6 copy-start.26
  90.2 2.2 copy-start.25
  92.2 7.9 copy-start.61
  92.2 11.1 %copy-start.59 = (s32[256]{0:T(256)S(1)}, s32[256]{0:T(256)}, u32[]{:S(2)}) copy-start(s32[256]{0:T(256)} %get-tuple-element.68) | copy-start | bytes 3076
  93.9 2.9 collective-permute-start
  98.6 84.4 %collective-permute-start.1 = (bf16[2,2,256,1024]{3,2,0,1:T(8,128)(2,1)S(1)}, bf16[2,2,256,1024]{3,2,0,1:T(8,128)(2,1)}, u32[]{:S(2)}, u32[]{:S(2)}) collective-permute-start(bf16[2,2,256,1024]{3,2,0,1:T(8,128)(2,1)S(1)} %maximum_select_fusion.1), channel_id=1, source_target_pairs={{0,2},{1,3},{2,0},{3,1},{4,6},{5,7},{6,4},{7,5},{8,10},{9,11},{10,... | collective-permute-start | bytes 6291464 | tf_op jit(solution)/shard_map/ppermute | solution.py:13
  102.6 172.8 %copy-start.41 = (f32[256]{0:T(256)}, f32[256]{0:T(256)S(1)}, u32[]{:S(2)}) copy-start(f32[256]{0:T(256)S(1)} %and_convert_fusion) | copy-start | bytes 3076
  193.8 6.0 copy-start.23
  202.0 9.7 %copy-start.8 = (f32[4,256,1024]{2,1,0:T(8,128)}, f32[4,256,1024]{2,1,0:T(8,128)S(1)}, u32[]{:S(2)}) copy-start(f32[4,256,1024]{2,1,0:T(8,128)S(1)} %get-tuple-element.50) | copy-start | bytes 12582916
  202.0 9.7 %copy-start.51 = (f32[4,256]{1,0:T(4,128)}, f32[4,256]{1,0:T(4,128)S(1)}, u32[]{:S(2)}) copy-start(f32[4,256]{1,0:T(4,128)S(1)} %get-tuple-element.49) | copy-start | bytes 12292
  202.0 3.1 copy-start.27
  205.1 6.6 copy-start.53
  206.2 8.6 %copy-start.3 = (f32[4,256,1024]{2,1,0:T(8,128)}, f32[4,256,1024]{2,1,0:T(8,128)S(1)}, u32[]{:S(2)}) copy-start(f32[4,256,1024]{2,1,0:T(8,128)S(1)} %get-tuple-element.52) | copy-start | bytes 12582916
  206.2 8.6 %copy-start.54 = (f32[4,256]{1,0:T(4,128)}, f32[4,256]{1,0:T(4,128)S(1)}, u32[]{:S(2)}) copy-start(f32[4,256]{1,0:T(4,128)S(1)} %get-tuple-element.51) | copy-start | bytes 12292
  207.3 7.5 copy-start.55
  208.4 7.5 copy-start
  208.4 7.5 copy-start.56
  209.5 6.4 copy-start.57
  210.6 6.3 copy-start.5
  210.6 6.3 copy-start.49
  210.6 3.1 copy-start.18
  213.7 3.2 copy-start.50
  217.0 1.9 copy-start.32
  218.0 43.9 %copy-start.11 = (bf16[256,1024]{1,0:T(8,128)(2,1)S(1)}, bf16[256,1024]{1,0:T(8,128)(2,1)}, u32[]{:S(2)}) copy-start(bf16[256,1024]{1,0:T(8,128)(2,1)} %param.12) | copy-start | bytes 1572868
  221.1 351.7 %reduce-scatter.11.cloned.1.call-start = ((), (), s32[]{:S(2)}) async-start(), calls=%async_computation.11 | async-start | bytes 9437184 | tf_op jit(solution)/shard_map/reduce_scatter | solution.py:309
  267.8 2.0 copy-start.63
  275.3 4.5 copy-start.52
  275.3 342.2 %reduce-scatter.9.cloned.1.call-start = ((), (), s32[]{:S(2)}) async-start(), calls=%async_computation.10 | async-start | bytes 9437184 | tf_op jit(solution)/shard_map/reduce_scatter | solution.py:303
  321.6 9.6 %copy-start.44 = (f32[256]{0:T(256)S(1)}, f32[256]{0:T(256)}, u32[]{:S(2)}) copy-start(f32[256]{0:T(256)} %copy-done.43) | copy-start | bytes 3076
  321.6 9.6 %copy-start.47 = (f32[256]{0:T(256)S(1)}, f32[256]{0:T(256)}, u32[]{:S(2)}) copy-start(f32[256]{0:T(256)} %copy-done.46) | copy-start | bytes 3076
  336.9 350.8 %reduce-scatter.5.cloned.1.call-start = ((), (), s32[]{:S(2)}) async-start(), calls=%async_computation.8 | async-start | bytes 7077888 | tf_op jit(solution)/shard_map/reduce_scatter | solution.py:297
  337.0 4.1 copy-start.1
  337.8 4.1 copy-start.39
  341.1 2.2 copy-start.6
  352.9 3.9 copy-start.9
  352.9 3.9 copy-start.38
  356.8 2.3 copy-start.4
  356.8 3.0 copy-start.19
  361.3 3.0 copy-start.7
  361.3 2.9 copy-start.40
  362.2 3.7 copy-start.12
  365.9 3.0 copy-start.2
  366.7 3.7 copy-start.14
  381.5 3.5 copy-start.10
  386.7 170.4 %collective-permute-start.2 = (f32[2,2,256,1024]{2,3,1,0:T(8,128)S(1)}, f32[2,2,256,1024]{2,3,1,0:T(8,128)S(1)}, u32[]{:S(2)}, u32[]{:S(2)}) collective-permute-start(f32[2,2,256,1024]{2,3,1,0:T(8,128)S(1)} %slice_select_fusion), channel_id=1, source_target_pairs={{0,2},{1,3},{2,0},{3,1},{4,6},{5,7},{6,4},{7,5},{8,10},{9,11},{10,... | collective-permute-start | bytes 12582920 | tf_op jit(solution)/shard_map/ppermute | solution.py:13
  558.2 2.1 copy-start.13
  558.2 6.2 collective-permute-start.3
  560.3 1.6 copy-start.15
  570.2 2.5 copy-start.60
  570.2 206.4 %all-reduce.13.cloned.1.call-start = ((), (), s32[]{:S(2)}) async-start(), calls=%async_computation.12 | async-start | bytes 6291456 | tf_op jit(solution)/shard_map/psum | solution.py:319
  687.8 7.6 copy-start.21
  687.8 7.6 copy-start.29
  687.8 7.6 copy-start.42
  695.3 1.7 copy-start.31
  702.8 5.1 copy-start.33
  702.8 6.5 copy-start.58
  776.7 7.1 copy-start.34
  (13 other events, 13.6 us)
Sparse Core Ops, SparseCore 0:
  11.0 72.3 all-gather.5
  86.3 95.9 all-gather.9
  185.3 57.3 all-gather.7
  245.6 75.9 all-gather.11
  323.7 34.5 reduce-scatter.6
  360.4 144.0 reduce-scatter.10
  506.8 110.6 reduce-scatter.8
  619.8 67.8 reduce-scatter.4
  691.1 85.5 all-reduce.12
where the time goes:
time: 800 us; the launch traced here: 792 us
  waiting for transfers between devices  453 us (57%)
  blocking collectives  120 us (15%)
  matrix products  92.3 us (12%)
  local copies, waits for them, and re-layouts  61.9 us (8%)
  other arithmetic  43.2 us (5%)
  between operations  18 us (2%)
    ppermute x4, waiting for transfers between devices, swapped(): lax.ppermute(array, axis, [(i, i ^ 1 << distance) for i in range(lax.axis...  250 us
    reduce_scatter x1, waiting for transfers between devices, local(): lax.psum_scatter(gradients[2].astype(jnp.bfloat16), 'dev', scatter_dimens...  70.2 us
    unnamed x2, blocking collectives  69.3 us
    reduce_scatter x1, waiting for transfers between devices, local(): lax.psum_scatter(gradients[4].astype(jnp.bfloat16), 'dev', scatter_dimens...  44.7 us
    all_gather x1, blocking collectives, local(): lax.all_gather(b_fc1, ('grp', 'dev'), axis=0, tiled=True)  40.2 us
    all_gather x1, waiting for transfers between devices, local(): lax.all_gather(w_fc2, ('grp', 'dev'), axis=0, tiled=True)  35.7 us
    unnamed x140, local copies, waits for them, and re-layouts  28.3 us
    psum x1, waiting for transfers between devices, local(): lax.psum(shares[2].astype(jnp.bfloat16), 'grp').astype(jnp.float32)  27.6 us
  transfers between devices with their start and end apart: 13, of which 8 were waited for; matrix products, arithmetic and copies ran while one was open for 21% of the time, Pallas kernels for 0%

commit v1 on v0

--- a/solution.py
+++ b/solution.py
@@ -316,7 +316,7 @@
     summed = (
         lax.psum(shares[0].astype(jnp.bfloat16), "grp").astype(jnp.float32),
         lax.psum(shares[1].astype(jnp.bfloat16), "grp").astype(jnp.float32),
-        lax.psum(shares[2].astype(jnp.bfloat16), "grp").astype(jnp.float32),
+        jnp.sum(lax.all_gather(shares[2].astype(jnp.bfloat16), "grp"), axis=0).astype(jnp.float32),
         lax.psum(shares[3].astype(jnp.bfloat16), "grp").astype(jnp.float32),
         lax.psum(shares[4].astype(jnp.bfloat16), "grp").astype(jnp.float32),
         lax.psum(shares[5].astype(jnp.bfloat16), "grp").astype(jnp.float32),

time: 800 us -> 828 us (1.035)
  waiting for transfers between devices: 453 us -> 481 us
    all_gather x0 -> x1, waiting for transfers between devices: none -> 39.3 us  [local(): lax.all_gather(shares[2].astype(jnp.bfloat16), 'grp')]
    psum x1, waiting for transfers between devices: 27.6 us -> 13.6 us  [local(): lax.psum(shares[3].astype(jnp.bfloat16), 'grp').astype(jnp.float32)]
  transfers between devices with their start and end apart: 13 -> 14, of which waited for: 8 -> 9; matrix products, arithmetic and copies ran while one was open for 21% -> 21% of each run, Pallas kernels for 0% -> 0%
where the time goes in v1:
time: 828 us; the launch traced here: 820 us
  waiting for transfers between devices  481 us (58%)
  blocking collectives  119 us (14%)
  matrix products  92.3 us (11%)
  local copies, waits for them, and re-layouts  61.4 us (7%)
  other arithmetic  44.6 us (5%)
  between operations  18.3 us (2%)
    ppermute x4, waiting for transfers between devices, swapped(): lax.ppermute(array, axis, [(i, i ^ 1 << distance) for i in range(lax.axis...  250 us
    reduce_scatter x1, waiting for transfers between devices, local(): lax.psum_scatter(gradients[2].astype(jnp.bfloat16), 'dev', scatter_dimens...  69.9 us
    unnamed x2, blocking collectives  68.8 us
    reduce_scatter x1, waiting for transfers between devices, local(): lax.psum_scatter(gradients[4].astype(jnp.bfloat16), 'dev', scatter_dimens...  47.2 us
    all_gather x1, blocking collectives, local(): lax.all_gather(b_fc1, ('grp', 'dev'), axis=0, tiled=True)  40.2 us
    all_gather x1, waiting for transfers between devices, local(): lax.all_gather(shares[2].astype(jnp.bfloat16), 'grp')  39.3 us
    all_gather x1, waiting for transfers between devices, local(): lax.all_gather(w_fc2, ('grp', 'dev'), axis=0, tiled=True)  35.7 us
    unnamed x140, local copies, waits for them, and re-layouts  27.8 us
  transfers between devices with their start and end apart: 14, of which 9 were waited for; matrix products, arithmetic and copies ran while one was open for 21% of the time, Pallas kernels for 0%

profile of v1, /device:TPU:0, one launch (start us, length us, event | category | flops | bytes accessed | tf_op | source)
XLA Modules:
  0.0 820.4 jit_solution(7519158692845826115)
XLA Ops:
  12.6 42.4 %all-reduce.7 = (bf16[1024]{0:T(1024)(128)(2,1)}, bf16[1024]{0:T(1024)(128)(2,1)S(1)}, bf16[1024]{0:T(1024)(128)(2,1)S(1)}) all-reduce(bf16[1024]{0:T(1024)(128)(2,1)S(1)} %dynamic-update-slice.2, bf16[1024]{0:T(1024)(128)(2,1)S(1)} %dynamic-update-slice.1, ...), channel_id=1, replica_groups=mesh['grp'=4,'dev'=8] {'grp','dev'}, use_global_device_ids=true, to_apply=%add.2 | all-reduce | flops 3072 | bytes 12288
  58.7 1.5 fusion.76
  61.0 22.4 %all-gather.8.cloned.1.call-done = bf16[1024,3072]{1,0:T(8,128)(2,1)} async-done(((bf16[32,3072]{1,0:T(8,128)(2,1)}), bf16[1024,3072]{1,0:T(8,128)(2,1)}) %all-gather.8.cloned.1.call-update) | async-done | bytes 6291472 | tf_op jit(solution)/shard_map/all_gather | solution.py:185
  83.4 4.9 fusion.118
  88.4 1.5 copy-done.26
  90.6 1.5 subtract_convert_fusion.2
  92.4 1.3 fusion.79
  94.2 2.5 collective-permute-done
  96.8 1.9 maximum_select_fusion.1
  98.6 1.4 collective-permute-start.1
  104.8 78.3 %collective-permute-done.1 = bf16[2,2,256,1024]{3,2,0,1:T(8,128)(2,1)} collective-permute-done((bf16[2,2,256,1024]{3,2,0,1:T(8,128)(2,1)S(1)}, bf16[2,2,256,1024]{3,2,0,1:T(8,128)(2,1)}, u32[]{:S(2)}, u32[]{:S(2)}) %collective-permute-start.1) | collective-permute-done | bytes 2097184 | tf_op jit(solution)/shard_map/ppermute | solution.py:13
  183.1 2.5 maximum_select_fusion
  185.6 2.4 fusion.120
  188.1 3.0 copy.55
  191.1 2.7 reshape_squeeze.10
  193.8 3.1 copy.53
  196.9 2.9 reshape_squeeze.9
  199.8 2.2 fusion.122
  203.1 2.0 copy-done.27
  211.7 2.0 copy-done.18
  218.9 2.2 convolution_convert_fusion.3
  221.2 40.2 %all-gather.1 = bf16[32,1,128]{2,1,0:T(2,128)(2,1)S(1)} all-gather(bf16[1,1,128]{2,1,0:T(2,128)(2,1)} %bitcast.119), channel_id=1, replica_groups=mesh['grp'=4,'dev'=8] {'grp','dev'}, dimensions={0}, use_global_device_ids=true | all-gather | bytes 8448 | tf_op jit(solution)/shard_map/all_gather | solution.py:188
  262.0 5.9 convolution_add_fusion
  267.9 2.0 copy-done.63
  269.8 5.5 convolution_convert_fusion
  275.4 3.2 convolution_convert_fusion.4
  281.9 4.0 fusion.40
  285.9 35.7 %all-gather.14.cloned.1.call-done = bf16[4096,1024]{1,0:T(8,128)(2,1)} async-done(((bf16[128,1024]{1,0:T(8,128)(2,1)}), bf16[4096,1024]{1,0:T(8,128)(2,1)}) %all-gather.14.cloned.1.call-update) | async-done | bytes 8388624 | tf_op jit(solution)/shard_map/all_gather | solution.py:189
  321.6 8.2 %fusion.126 = (bf16[4096]{0:T(1024)(128)(2,1)}, bf16[256,4096]{1,0:T(8,128)(2,1)S(1)}) fusion(f32[256,4096]{1,0:T(8,128)} %copy-done.63, bf16[4096,1024]{1,0:T(8,128)(2,1)} %all-gather.14.cloned.1.call-done, bf16[256,1024]{1,0:T(8,128)(2,1)} %param.13, f32[256]{0:T(256)} %copy-done.41), kind=kOutput, calls=%fused_computation.212 | convolution fusion | flops 2169237504 | bytes 15213568 | tf_op jit(solution)/shard_map/re,fe->rf/dot_general | solution.py:242
  329.8 1.3 copy-done.30
  331.1 5.8 convolution_convert_fusion.1
  337.8 3.2 fusion.37
  341.9 1.4 copy-done.6
  344.5 2.6 pad_maximum_fusion.1
  347.1 5.8 stack.16
  352.9 3.9 multiply_reduce_fusion
  359.7 1.6 multiply_reduce_fusion.1
  362.7 1.6 copy-done.7
  364.3 1.6 multiply_reduce_fusion.3
  367.2 1.6 copy-done.2
  368.8 1.6 multiply_reduce_fusion.2
  371.3 1.3 copy-done.16
  373.1 2.5 pad_maximum_fusion
  375.6 5.8 stack.15
  381.5 3.1 copy_dynamic-update-slice_fusion.1
  386.7 1.6 collective-permute-start.2
  388.3 168.8 %collective-permute-done.2 = f32[2,2,256,1024]{2,3,1,0:T(8,128)S(1)} collective-permute-done((f32[2,2,256,1024]{2,3,1,0:T(8,128)S(1)}, f32[2,2,256,1024]{2,3,1,0:T(8,128)S(1)}, u32[]{:S(2)}, u32[]{:S(2)}) %collective-permute-start.2) | collective-permute-done | bytes 4194336 | tf_op jit(solution)/shard_map/ppermute | solution.py:13
  565.5 4.6 convolution_convert_fusion.2
  570.3 47.2 %reduce-scatter.9.cloned.1.call-done = bf16[128,4096]{1,0:T(8,128)(2,1)} async-done(((bf16[1024,4096]{1,0:T(8,128)(2,1)}), bf16[128,4096]{1,0:T(8,128)(2,1)}) %reduce-scatter.9.cloned.1.call-update) | async-done | bytes 1048592 | tf_op jit(solution)/shard_map/reduce_scatter | solution.py:303
  617.8 69.9 %reduce-scatter.5.cloned.1.call-done = bf16[128,3072]{1,0:T(8,128)(2,1)} async-done(((bf16[1024,3072]{1,0:T(8,128)(2,1)}), bf16[128,3072]{1,0:T(8,128)(2,1)}) %reduce-scatter.5.cloned.1.call-update) | async-done | bytes 786448 | tf_op jit(solution)/shard_map/reduce_scatter | solution.py:297
  689.7 7.5 convolution_add_fusion.2
  697.3 1.6 fusion.49
  698.9 5.8 fusion.127
  704.7 5.1 fusion.75
  709.8 1.3 fusion.77
  711.1 26.3 %all-reduce.8 = (bf16[1024]{0:T(1024)(128)(2,1)S(1)}, bf16[1024]{0:T(1024)(128)(2,1)S(1)}, bf16[4096]{0:T(1024)(128)(2,1)S(1)}, bf16[1024]{0:T(1024)(128)(2,1)S(1)}) all-reduce(bf16[1024]{0:T(1024)(128)(2,1)S(1)} %get-tuple-element.10, bf16[1024]{0:T(1024)(128)(2,1)S(1)} %get-tuple-element.13, ...), channel_id=3, replica_groups=mesh['grp'=4,'dev'=8] {'dev'}, use_global_device_ids=true, to_apply=%region_17.18.clone | all-reduce | flops 7168 | bytes 28672
  737.8 10.2 %all-reduce.9 = (bf16[128]{0:T(256)(128)(2,1)S(1)}, bf16[128]{0:T(256)(128)(2,1)S(1)}, bf16[512]{0:T(512)(128)(2,1)S(1)}, bf16[128]{0:T(256)(128)(2,1)S(1)}) all-reduce(bf16[128]{0:T(256)(128)(2,1)S(1)} %dynamic-slice.1, bf16[128]{0:T(256)(128)(2,1)S(1)} %dynamic-slice.3, ...), channel_id=1, replica_groups=mesh['grp'=4,'dev'=8] {'grp'}, use_global_device_ids=true, to_apply=%region_18.19 | all-reduce | flops 896 | bytes 3584 | tf_op jit(solution)/shard_map/psum | solution.py:317
  750.1 13.6 %all-reduce.13.cloned.1.call-done = (bf16[128,1024]{1,0:T(8,128)(2,1)}, bf16[128,4096]{1,0:T(8,128)(2,1)}, bf16[512,1024]{1,0:T(8,128)(2,1)}) async-done(((bf16[128,1024]{1,0:T(8,128)(2,1)}, bf16[128,4096]{1,0:T(8,128)(2,1)}, bf16[512,1024]{1,0:T(8,128)(2,1)}), (bf16[128,1024]{1,0:T(8,128)(2,1)}, bf16[128,4096]{1,0:T(8,128)(2,1)}, bf16[512,1024]{1,0:T(8,128)(2,1)})) %all-reduce.13.cloned.1.call-update) | async-done | bytes 2359312 | tf_op jit(solution)/shard_map/psum | solution.py:320
  763.7 1.9 convert_element_type.209
  765.6 2.8 convert_element_type.211
  768.4 1.6 convert_element_type.214
  769.9 39.3 %all-gather.16.cloned.1.call-done = bf16[512,3072]{1,0:T(8,128)(2,1)} async-done(((bf16[128,3072]{1,0:T(8,128)(2,1)}), bf16[512,3072]{1,0:T(8,128)(2,1)}) %all-gather.16.cloned.1.call-update) | async-done | bytes 3145744 | tf_op jit(solution)/shard_map/all_gather | solution.py:319
  809.3 2.5 reduce_sum.173
  811.8 1.3 convert_element_type.207
  (231 shorter events, 55.1 us)
Async XLA Ops:
  7.2 76.2 %all-gather.8.cloned.1.call-start = ((), (), s32[]{:S(2)}) async-start(), calls=%async_computation.4 | async-start | bytes 6488064 | tf_op jit(solution)/shard_map/all_gather | solution.py:185
  7.9 254.1 %all-gather.12.cloned.1.call-start = ((), (), s32[]{:S(2)}) async-start(), calls=%async_computation.6 | async-start | bytes 8650752 | tf_op jit(solution)/shard_map/all_gather | solution.py:187
  8.7 266.7 %all-gather.10.cloned.1.call-start = ((), (), s32[]{:S(2)}) async-start(), calls=%async_computation.5 | async-start | bytes 2162688 | tf_op jit(solution)/shard_map/all_gather | solution.py:186
  9.4 312.2 %all-gather.14.cloned.1.call-start = ((), (), s32[]{:S(2)}) async-start(), calls=%async_computation.7 | async-start | bytes 8650752 | tf_op jit(solution)/shard_map/all_gather | solution.py:189
  10.0 560.3 %reduce-scatter.7.cloned.1.call-start = ((), (), s32[]{:S(2)}) async-start(), calls=%async_computation.9 | async-start | bytes 2359296 | tf_op jit(solution)/shard_map/reduce_scatter | solution.py:300
  58.7 203.3 %copy-start.43 = (f32[256]{0:T(256)}, f32[256]{0:T(256)S(1)}, u32[]{:S(2)}) copy-start(f32[256]{0:T(256)S(1)} %broadcast_multiply_fusion.2) | copy-start | bytes 3076
  60.2 28.0 %copy-start.46 = (f32[256]{0:T(256)}, f32[256]{0:T(256)S(1)}, u32[]{:S(2)}) copy-start(f32[256]{0:T(256)S(1)} %add_rsqrt_fusion) | copy-start | bytes 3076
  90.2 2.2 copy-start.25
  92.2 7.9 copy-start.61
  92.2 11.1 %copy-start.59 = (s32[256]{0:T(256)S(1)}, s32[256]{0:T(256)}, u32[]{:S(2)}) copy-start(s32[256]{0:T(256)} %get-tuple-element.67) | copy-start | bytes 3076
  93.9 2.9 collective-permute-start
  98.6 84.4 %collective-permute-start.1 = (bf16[2,2,256,1024]{3,2,0,1:T(8,128)(2,1)S(1)}, bf16[2,2,256,1024]{3,2,0,1:T(8,128)(2,1)}, u32[]{:S(2)}, u32[]{:S(2)}) collective-permute-start(bf16[2,2,256,1024]{3,2,0,1:T(8,128)(2,1)S(1)} %maximum_select_fusion.1), channel_id=1, source_target_pairs={{0,2},{1,3},{2,0},{3,1},{4,6},{5,7},{6,4},{7,5},{8,10},{9,11},{10,... | collective-permute-start | bytes 6291464 | tf_op jit(solution)/shard_map/ppermute | solution.py:13
  102.6 172.8 %copy-start.41 = (f32[256]{0:T(256)}, f32[256]{0:T(256)S(1)}, u32[]{:S(2)}) copy-start(f32[256]{0:T(256)S(1)} %and_convert_fusion) | copy-start | bytes 3076
  193.8 6.0 copy-start.23
  202.0 9.7 %copy-start.8 = (f32[4,256,1024]{2,1,0:T(8,128)}, f32[4,256,1024]{2,1,0:T(8,128)S(1)}, u32[]{:S(2)}) copy-start(f32[4,256,1024]{2,1,0:T(8,128)S(1)} %get-tuple-element.49) | copy-start | bytes 12582916
  202.0 9.7 %copy-start.51 = (f32[4,256]{1,0:T(4,128)}, f32[4,256]{1,0:T(4,128)S(1)}, u32[]{:S(2)}) copy-start(f32[4,256]{1,0:T(4,128)S(1)} %get-tuple-element.48) | copy-start | bytes 12292
  202.0 3.1 copy-start.27
  205.1 6.6 copy-start.53
  206.2 8.6 %copy-start.3 = (f32[4,256,1024]{2,1,0:T(8,128)}, f32[4,256,1024]{2,1,0:T(8,128)S(1)}, u32[]{:S(2)}) copy-start(f32[4,256,1024]{2,1,0:T(8,128)S(1)} %get-tuple-element.51) | copy-start | bytes 12582916
  206.2 8.6 %copy-start.54 = (f32[4,256]{1,0:T(4,128)}, f32[4,256]{1,0:T(4,128)S(1)}, u32[]{:S(2)}) copy-start(f32[4,256]{1,0:T(4,128)S(1)} %get-tuple-element.50) | copy-start | bytes 12292
  207.3 7.5 copy-start.55
  208.4 7.5 copy-start
  208.4 7.5 copy-start.56
  209.5 6.4 copy-start.57
  210.6 6.3 copy-start.5
  210.6 6.3 copy-start.49
  210.6 3.1 copy-start.18
  213.7 3.2 copy-start.50
  217.0 1.9 copy-start.32
  218.0 43.9 %copy-start.11 = (bf16[256,1024]{1,0:T(8,128)(2,1)S(1)}, bf16[256,1024]{1,0:T(8,128)(2,1)}, u32[]{:S(2)}) copy-start(bf16[256,1024]{1,0:T(8,128)(2,1)} %param.12) | copy-start | bytes 1572868
  221.1 349.2 %reduce-scatter.11.cloned.1.call-start = ((), (), s32[]{:S(2)}) async-start(), calls=%async_computation.11 | async-start | bytes 9437184 | tf_op jit(solution)/shard_map/reduce_scatter | solution.py:309
  267.8 2.0 copy-start.63
  275.3 4.5 copy-start.52
  275.3 342.2 %reduce-scatter.9.cloned.1.call-start = ((), (), s32[]{:S(2)}) async-start(), calls=%async_computation.10 | async-start | bytes 9437184 | tf_op jit(solution)/shard_map/reduce_scatter | solution.py:303
  321.6 9.6 %copy-start.44 = (f32[256]{0:T(256)S(1)}, f32[256]{0:T(256)}, u32[]{:S(2)}) copy-start(f32[256]{0:T(256)} %copy-done.43) | copy-start | bytes 3076
  321.6 9.6 %copy-start.47 = (f32[256]{0:T(256)S(1)}, f32[256]{0:T(256)}, u32[]{:S(2)}) copy-start(f32[256]{0:T(256)} %copy-done.46) | copy-start | bytes 3076
  336.9 350.8 %reduce-scatter.5.cloned.1.call-start = ((), (), s32[]{:S(2)}) async-start(), calls=%async_computation.8 | async-start | bytes 7077888 | tf_op jit(solution)/shard_map/reduce_scatter | solution.py:297
  337.0 4.1 copy-start.1
  337.8 4.1 copy-start.39
  341.1 2.2 copy-start.6
  352.9 3.9 copy-start.9
  352.9 3.9 copy-start.38
  356.8 2.3 copy-start.4
  356.8 3.0 copy-start.19
  361.3 3.0 copy-start.7
  361.3 2.9 copy-start.40
  362.2 3.7 copy-start.12
  365.9 3.0 copy-start.2
  366.7 3.7 copy-start.14
  381.5 3.5 copy-start.10
  386.7 170.4 %collective-permute-start.2 = (f32[2,2,256,1024]{2,3,1,0:T(8,128)S(1)}, f32[2,2,256,1024]{2,3,1,0:T(8,128)S(1)}, u32[]{:S(2)}, u32[]{:S(2)}) collective-permute-start(f32[2,2,256,1024]{2,3,1,0:T(8,128)S(1)} %slice_select_fusion), channel_id=1, source_target_pairs={{0,2},{1,3},{2,0},{3,1},{4,6},{5,7},{6,4},{7,5},{8,10},{9,11},{10,... | collective-permute-start | bytes 12582920 | tf_op jit(solution)/shard_map/ppermute | solution.py:13
  558.2 2.1 copy-start.13
  558.2 6.2 collective-permute-start.3
  560.3 1.6 copy-start.15
  570.2 117.6 %copy-start.62 = (u32[32]{0:T(128)S(1)}, u32[32]{0:T(128)}, u32[]{:S(2)}) copy-start(u32[32]{0:T(128)} %constant.185) | copy-start | bytes 388
  570.2 119.5 %copy-start.60 = (bf16[1024]{0:T(1024)(128)(2,1)S(1)}, bf16[1024]{0:T(1024)(128)(2,1)}, u32[]{:S(2)}) copy-start(bf16[1024]{0:T(1024)(128)(2,1)} %get-tuple-element.14) | copy-start | bytes 6148
  570.2 193.5 %all-reduce.13.cloned.1.call-start = ((), (), s32[]{:S(2)}) async-start(), calls=%async_computation.13 | async-start | bytes 4718592 | tf_op jit(solution)/shard_map/psum | solution.py:320
  617.5 191.8 %all-gather.16.cloned.1.call-start = ((), (), s32[]{:S(2)}) async-start(), calls=%async_computation.12 | async-start | bytes 3932160 | tf_op jit(solution)/shard_map/all_gather | solution.py:319
  689.7 7.6 copy-start.21
  689.7 7.6 copy-start.29
  689.7 7.6 copy-start.42
  704.6 5.2 copy-start.33
  704.7 6.5 copy-start.58
  763.7 4.6 copy-start.34
  (14 other events, 16.2 us)
Sparse Core Ops, SparseCore 0:
  11.0 72.3 all-gather.7
  86.3 95.9 all-gather.11
  185.3 57.3 all-gather.9
  245.6 75.9 all-gather.13
  323.7 34.5 reduce-scatter.6
  360.4 144.0 reduce-scatter.10
  506.8 110.6 reduce-scatter.8
  619.8 67.8 reduce-scatter.4
  691.1 72.5 all-reduce.12
  765.4 43.8 all-gather.15
